TPU v7x, 32 devices: a whole 2x2x4 slice. The times are simulated.
32 devices in a mesh: grp: 4 (over z), wr: 8 (over y, x, core).
Axes of the slice: x: 2, y: 2, z: 4, core: 2. Of those that a mesh axis runs over, the one named last changes fastest.
Arguments:
- snapshots: float32 [256, 131072], P('wr', 'grp'), may hold values from -1300 to 1300
Outputs:
- basis: float32 [256, 131072], P(None, ('grp', 'wr'))
- r_scaled: float32 [256, 256], P(None, 'wr')
All inputs are finite; a program needn't handle non-finite values.
Results may differ from a plain program's by a relative error of at most 0.000073.
Values sent between devices are 32-bit elements; how exact they have to be, the bound alone decides.
No kernel may reach another device: no remote copies, remote signals or barrier semaphores. Data moves between devices by JAX's collectives and lax.ppermute only.
A program may use at most 64 MiB of HBM per device.

v0:
```python
import jax
import jax.numpy as jnp
from jax import lax
from jax.sharding import PartitionSpec as P


def partner(value, axis, stride):
    return lax.ppermute(value, axis, [(i, i ^ 1 << stride) for i in range(lax.axis_size(axis))])


def products(left, right):
    return lax.dot_general(
        left,
        right,
        (((1,), (1,)), ((), ())),
        precision=lax.Precision.HIGHEST,
        preferred_element_type=jnp.float32,
    )


def writer_levels(gram):
    for bit in range(lax.axis_size("wr").bit_length() - 1):
        gram = gram + partner(gram, "wr", bit)
    return gram


def group_levels(gram):
    for bit in range(lax.axis_size("grp").bit_length() - 1):
        gram = gram + partner(gram, "grp", bit)
    return gram


def body(snapshots):
    regrouped = lax.all_to_all(snapshots, "wr", split_axis=1, concat_axis=0, tiled=True)
    local_gram = products(regrouped, regrouped)
    total = writer_levels(group_levels(local_gram))
    lower = jnp.linalg.cholesky(total)
    cell_count = regrouped.shape[1] * lax.axis_size("grp") * lax.axis_size("wr")
    scale = jnp.sqrt(jnp.float32(cell_count))
    solved = lax.linalg.triangular_solve(lower, regrouped, left_side=True, lower=True)
    width = lower.shape[0] // lax.axis_size("wr")
    start = lax.axis_index("wr") * width
    columns = lax.dynamic_slice_in_dim(lower.T, start, width, 1)
    return (solved * scale, columns / scale)


def solution(mesh):
    placed = (P("wr", "grp"),)
    return jax.shard_map(
        body,
        mesh=mesh,
        in_specs=placed,
        out_specs=(P(None, ("grp", "wr")), P(None, "wr")),
        check_vma=False,
    )
```

profile of v0, /device:TPU:0, one launch (start us, length us, event | category | flops | bytes accessed | tf_op | source)
XLA Modules:
  0.0 169.7 jit_solution(11626017769321562424)
XLA Ops:
  0.6 2.5 %copy.22 = f32[4,8,8,4096]{3,2,0,1:T(8,128)S(1)} copy(f32[4,8,8,4096]{3,2,1,0:T(8,128)} %bitcast.50) | data formatting | bytes 8388608 | tf_op jit(solution)/shard_map/all_to_all | solution.py:34
  3.1 54.0 %all_to_all.19 = f32[32,8,4096]{2,0,1:T(8,128)S(1)} all-to-all(f32[32,8,4096]{2,0,1:T(8,128)S(1)} %bitcast.47), channel_id=1, replica_groups=mesh['grp'=4,'wr'=8] {'wr'}, dimensions={1} | all-to-all | bytes 8388608 | tf_op jit(solution)/shard_map/all_to_all | solution.py:34
  57.1 0.0 copy-start
  57.1 3.5 %fusion.10 = f32[256,256]{0,1:T(8,128)S(1)} fusion(f32[256,4096]{1,0:T(8,128)S(1)} %bitcast.45), kind=kOutput, calls=%fused_computation.32 | convolution fusion | flops 3221225472 | bytes 4456448 | tf_op jit(solution)/shard_map/dot_general | solution.py:12
  60.7 0.0 copy-done
  60.7 1.6 collective-permute-start
  62.3 5.9 %collective-permute-done = f32[256,256]{0,1:T(8,128)S(1)} collective-permute-done((f32[256,256]{0,1:T(8,128)S(1)}, f32[256,256]{0,1:T(8,128)S(1)}, u32[]{:S(2)}, u32[]{:S(2)}) %collective-permute-start) | collective-permute-done | bytes 262176 | tf_op jit(solution)/shard_map/ppermute | solution.py:8
  68.3 2.7 %collective-permute-start.1 = (f32[256,256]{0,1:T(8,128)S(1)}, f32[256,256]{0,1:T(8,128)S(1)}, u32[]{:S(2)}, u32[]{:S(2)}) collective-permute-start(f32[256,256]{0,1:T(8,128)S(1)} %add.40), channel_id=1, source_target_pairs={{0,16},{8,24},{16,0},{24,8},{1,17},{9,25},{17,1},{25,9},{2,18},{10... | collective-permute-start | bytes 786440 | tf_op jit(solution)/shard_map/ppermute | solution.py:8
  70.9 10.6 %collective-permute-done.1 = f32[256,256]{0,1:T(8,128)S(1)} collective-permute-done((f32[256,256]{0,1:T(8,128)S(1)}, f32[256,256]{0,1:T(8,128)S(1)}, u32[]{:S(2)}, u32[]{:S(2)}) %collective-permute-start.1) | collective-permute-done | bytes 262176 | tf_op jit(solution)/shard_map/ppermute | solution.py:8
  81.5 0.1 collective-permute-start.2
  81.6 1.5 collective-permute-done.2
  83.2 1.8 %collective-permute-start.3 = (f32[256,256]{0,1:T(8,128)S(1)}, f32[256,256]{0,1:T(8,128)S(1)}, u32[]{:S(2)}, u32[]{:S(2)}) collective-permute-start(f32[256,256]{0,1:T(8,128)S(1)} %add.42), channel_id=1, source_target_pairs={{0,2},{1,3},{2,0},{3,1},{4,6},{5,7},{6,4},{7,5},{8,10},{9,11},{10,... | collective-permute-start | bytes 786440 | tf_op jit(solution)/shard_map/ppermute | solution.py:8
  85.0 6.6 %collective-permute-done.3 = f32[256,256]{0,1:T(8,128)S(1)} collective-permute-done((f32[256,256]{0,1:T(8,128)S(1)}, f32[256,256]{0,1:T(8,128)S(1)}, u32[]{:S(2)}, u32[]{:S(2)}) %collective-permute-start.3) | collective-permute-done | bytes 262176 | tf_op jit(solution)/shard_map/ppermute | solution.py:8
  91.7 0.6 collective-permute-start.4
  92.2 4.0 %fusion.9 = (f32[4,32,4096]{2,1,0:T(8,128)}, f32[4,32,4096]{2,1,0:T(8,128)S(1)}) fusion(f32[8,32,4096]{2,1,0:T(8,128)} %bitcast.46), kind=kLoop, calls=%fused_computation.31 | loop fusion | bytes 8388608 | tf_op jit(solution)/shard_map/triangular_solve | solution.py:40
  96.3 3.0 %collective-permute-done.4 = f32[256,256]{0,1:T(8,128)S(1)} collective-permute-done((f32[256,256]{0,1:T(8,128)S(1)}, f32[256,256]{0,1:T(8,128)S(1)}, u32[]{:S(2)}, u32[]{:S(2)}) %collective-permute-start.4) | collective-permute-done | bytes 262176 | tf_op jit(solution)/shard_map/ppermute | solution.py:8
  99.3 0.1 copy.18
  99.5 11.7 %cholesky.50 = f32[128,128]{1,0:T(8,128)S(1)} custom-call(f32[128,128]{1,0:T(8,128)S(1)} %cholesky.118), custom_call_target="Cholesky" | custom-call | tf_op jit(solution)/shard_map/jit(cholesky)/cholesky | solution.py:37
  111.3 9.8 %custom-call.14 = f32[1,128,128]{1,2,0:T(8,128)S(1)} custom-call(f32[1,128,128]{2,1,0:T(8,128)S(1)} %get-tuple-element.27), custom_call_target="InvertDiagBlocksLowerTriangular" | custom-call | tf_op jit(solution)/shard_map/jit(cholesky)/cholesky | solution.py:37
  121.1 0.2 constant_dynamic-update-slice_fusion
  121.3 0.3 slice_subtract_fusion
  121.6 11.9 %cholesky.105 = f32[128,128]{1,0:T(8,128)S(1)} custom-call(f32[128,128]{1,0:T(8,128)S(1)} %slice_subtract_fusion), custom_call_target="Cholesky" | custom-call | tf_op jit(solution)/shard_map/jit(cholesky)/cholesky | solution.py:37
  133.5 0.6 compare_reduce_fusion
  135.4 0.1 triangular_solve.61
  135.4 3.8 %while.1 = (s32[]{:T(128)}, f32[256,256]{1,0:T(8,128)S(1)}, s32[2,2]{1,0:T(2,128)S(1)}, f32[2,128,128]{2,1,0:T(8,128)S(1)}, s32[]{:T(128)}) while((s32[]{:T(128)}, f32[256,256]{1,0:T(8,128)S(1)}, s32[2,2]{1,0:T(2,128)S(1)}, f32[2,128,128]{2,1,0:T(8,128)S(1)}, s32[]{:T(128)}) %tuple.29), condition=%wide.while_cond, body=%wide.while_body.sunk | while | flops 2 | bytes 131189 | solution.py:40
  135.4 0.6 fusion.19
  136.0 1.3 bitcast_dynamic-update-slice_fusion.2
  137.3 0.6 fusion.19
  137.9 1.3 bitcast_dynamic-update-slice_fusion.2
  139.2 19.7 %custom-call.15 = f32[2,128,128]{1,2,0:T(8,128)S(1)} custom-call(f32[2,128,128]{2,1,0:T(8,128)S(1)} %get-tuple-element.9), custom_call_target="InvertDiagBlocksLowerTriangular" | custom-call | tf_op jit(solution)/shard_map/triangular_solve | solution.py:40
  158.9 3.5 %fusion.4 = f32[128,4096]{1,0:T(8,128)S(1)} fusion(f32[128,4096]{1,0:T(8,128)} %bitcast.49, f32[2,128,128]{1,2,0:T(8,128)S(1)} %custom-call.15), kind=kOutput, calls=%fused_computation.14 | convolution fusion | flops 805306368 | bytes 4259840 | tf_op jit(solution)/shard_map/triangular_solve | solution.py:40
  162.4 2.0 %convolution_subtract_fusion = f32[128,4096]{1,0:T(8,128)S(1)} fusion(f32[128,4096]{1,0:T(8,128)S(1)} %bitcast.48, f32[128,4096]{1,0:T(8,128)S(1)} %fusion.4, f32[256,256]{1,0:T(8,128)S(1)} %get-tuple-element.76), kind=kOutput, calls=%fused_computation.2 | convolution fusion | flops 805830656 | bytes 6356992 | tf_op jit(solution)/shard_map/triangular_solve | solution.py:40
  164.4 1.9 %fusion.3 = f32[128,4096]{1,0:T(8,128)S(1)} fusion(f32[128,4096]{1,0:T(8,128)S(1)} %convolution_subtract_fusion, f32[2,128,128]{1,2,0:T(8,128)S(1)} %custom-call.15), kind=kOutput, calls=%fused_computation.12 | convolution fusion | flops 805306368 | bytes 4259840 | tf_op jit(solution)/shard_map/triangular_solve | solution.py:40
  166.3 2.7 %maximum_multiply_fusion = f32[256,4096]{1,0:T(8,128)} fusion(f32[128,4096]{1,0:T(8,128)S(1)} %fusion.3, f32[128,4096]{1,0:T(8,128)S(1)} %fusion.4), kind=kLoop, calls=%fused_computation.4 | loop fusion | flops 2097152 | bytes 8388608 | tf_op jit(solution)/shard_map/mul | solution.py:44
  169.1 0.6 multiply_bitcast_fusion
  (15 shorter events, 0.4 us)
Async XLA Ops:
  57.1 3.5 %copy-start = (f32[32,8,4096]{2,0,1:T(8,128)}, f32[32,8,4096]{2,0,1:T(8,128)S(1)}, u32[]{:S(2)}) copy-start(f32[32,8,4096]{2,0,1:T(8,128)S(1)} %all_to_all.19) | copy-start | bytes 12582916
  60.7 7.6 %collective-permute-start = (f32[256,256]{0,1:T(8,128)S(1)}, f32[256,256]{0,1:T(8,128)S(1)}, u32[]{:S(2)}, u32[]{:S(2)}) collective-permute-start(f32[256,256]{0,1:T(8,128)S(1)} %fusion.10), channel_id=1, source_target_pairs={{0,8},{8,0},{16,24},{24,16},{1,9},{9,1},{17,25},{25,17},{2,10},{10... | collective-permute-start | bytes 786440 | tf_op jit(solution)/shard_map/ppermute | solution.py:8
  68.3 13.2 %collective-permute-start.1 = (f32[256,256]{0,1:T(8,128)S(1)}, f32[256,256]{0,1:T(8,128)S(1)}, u32[]{:S(2)}, u32[]{:S(2)}) collective-permute-start(f32[256,256]{0,1:T(8,128)S(1)} %add.40), channel_id=1, source_target_pairs={{0,16},{8,24},{16,0},{24,8},{1,17},{9,25},{17,1},{25,9},{2,18},{10... | collective-permute-start | bytes 786440 | tf_op jit(solution)/shard_map/ppermute | solution.py:8
  81.5 1.6 collective-permute-start.2
  83.2 8.5 %collective-permute-start.3 = (f32[256,256]{0,1:T(8,128)S(1)}, f32[256,256]{0,1:T(8,128)S(1)}, u32[]{:S(2)}, u32[]{:S(2)}) collective-permute-start(f32[256,256]{0,1:T(8,128)S(1)} %add.42), channel_id=1, source_target_pairs={{0,2},{1,3},{2,0},{3,1},{4,6},{5,7},{6,4},{7,5},{8,10},{9,11},{10,... | collective-permute-start | bytes 786440 | tf_op jit(solution)/shard_map/ppermute | solution.py:8
  91.7 7.6 %collective-permute-start.4 = (f32[256,256]{0,1:T(8,128)S(1)}, f32[256,256]{0,1:T(8,128)S(1)}, u32[]{:S(2)}, u32[]{:S(2)}) collective-permute-start(f32[256,256]{0,1:T(8,128)S(1)} %add.43), channel_id=1, source_target_pairs={{0,4},{1,5},{2,6},{3,7},{4,0},{5,1},{6,2},{7,3},{8,12},{9,13},{10,... | collective-permute-start | bytes 786440 | tf_op jit(solution)/shard_map/ppermute | solution.py:8
where the time goes:
time: 170 us
  other arithmetic  57.4 us (34%)
  blocking collectives  54 us (32%)
  waiting for transfers between devices  27.6 us (16%)
  matrix products  11.4 us (7%)
  local copies, waits for them, and re-layouts  10.5 us (6%)
  starting transfers between devices  6.8 us (4%)
  between operations  1.98 us (1%)
    all_to_all x1, blocking collectives, body(): lax.all_to_all(snapshots, 'wr', split_axis=1, concat_axis=0, tiled=True)  54 us
    another operation x6, other arithmetic, body(): lower = jnp.linalg.cholesky(total)  34.1 us
    ppermute x5, waiting for transfers between devices, partner(): lax.ppermute(value, axis, [(i, i ^ 1 << stride) for i in range(lax.axis_s...  27.6 us
    another operation x3, other arithmetic, body(): lax.linalg.triangular_solve(lower, regrouped, left_side=True, lower=True)  19.7 us
    another operation x3, matrix products, body(): lax.linalg.triangular_solve(lower, regrouped, left_side=True, lower=True)  7.4 us
    ppermute x5, starting transfers between devices, partner(): lax.ppermute(value, axis, [(i, i ^ 1 << stride) for i in range(lax.axis_s...  6.8 us
    another operation x2, local copies, waits for them, and re-layouts, body(): lax.linalg.triangular_solve(lower, regrouped, left_side=True, lower=True)  4.08 us
    another operation x6, local copies, waits for them, and re-layouts  3.75 us
  transfers between devices with their start and end apart: 5, of which 5 were waited for; matrix products, arithmetic and copies ran while one was open for 2% of the time, Pallas kernels for 0%

commit v1 on v0

--- a/solution.py
+++ b/solution.py
@@ -1,7 +1,19 @@
+import functools
 import jax
 import jax.numpy as jnp
 from jax import lax
 from jax.sharding import PartitionSpec as P
+from jax.lax import all_to_all, axis_size
+
+
+def _draft_plane(vector, lane_axis):
+    return jnp.concatenate(
+        all_to_all(jnp.stack(jnp.split(vector, axis_size(lane_axis), axis=1)), lane_axis, 0, 0),
+        axis=0,
+    )
+
+
+meet_shelves_on = functools.partial(_draft_plane, lane_axis="wr")
 
 
 def partner(value, axis, stride):
@@ -31,7 +43,7 @@
 
 
 def body(snapshots):
-    regrouped = lax.all_to_all(snapshots, "wr", split_axis=1, concat_axis=0, tiled=True)
+    regrouped = meet_shelves_on(snapshots)
     local_gram = products(regrouped, regrouped)
     total = writer_levels(group_levels(local_gram))
     lower = jnp.linalg.cholesky(total)

time: 170 us -> 177 us (1.041)
  local copies, waits for them, and re-layouts: 10.5 us -> 16.6 us
    unnamed x2 -> x9, local copies, waits for them, and re-layouts: 0.01 us -> 7.56 us
    all_to_all x1 -> x0, local copies, waits for them, and re-layouts: 2.47 us -> none  [body(): lax.all_to_all(snapshots, 'wr', split_axis=1, concat_axis=0, tiled=True)]
    another operation x6 -> x7, local copies, waits for them, and re-layouts: 3.75 us -> 4.83 us
where the time goes in v1:
time: 177 us; the launch traced here: 176 us
  other arithmetic  57.4 us (32%)
  blocking collectives  54 us (31%)
  waiting for transfers between devices  27.6 us (16%)
  local copies, waits for them, and re-layouts  16.6 us (9%)
  matrix products  11.4 us (6%)
  starting transfers between devices  6.8 us (4%)
  between operations  2.01 us (1%)
    all_to_all x1, blocking collectives, _draft_plane(): all_to_all(jnp.stack(jnp.split(vector, axis_size(lane_axis), axis=1)), la...  54 us
    another operation x6, other arithmetic, body(): lower = jnp.linalg.cholesky(total)  34.1 us
    ppermute x5, waiting for transfers between devices, partner(): lax.ppermute(value, axis, [(i, i ^ 1 << stride) for i in range(lax.axis_s...  27.6 us
    another operation x3, other arithmetic, body(): lax.linalg.triangular_solve(lower, regrouped, left_side=True, lower=True)  19.7 us
    unnamed x9, local copies, waits for them, and re-layouts  7.56 us
    another operation x3, matrix products, body(): lax.linalg.triangular_solve(lower, regrouped, left_side=True, lower=True)  7.4 us
    ppermute x5, starting transfers between devices, partner(): lax.ppermute(value, axis, [(i, i ^ 1 << stride) for i in range(lax.axis_s...  6.8 us
    another operation x2, local copies, waits for them, and re-layouts, body(): lax.linalg.triangular_solve(lower, regrouped, left_side=True, lower=True)  4.08 us
  transfers between devices with their start and end apart: 5, of which 5 were waited for; matrix products, arithmetic and copies ran while one was open for 2% of the time, Pallas kernels for 0%

profile of v1, /device:TPU:0, one launch (start us, length us, event | category | flops | bytes accessed | tf_op | source)
XLA Modules:
  0.0 175.9 jit_solution(10119740545232719052)
XLA Ops:
  0.6 1.1 bitcast_dynamic-update-slice_fusion.8
  1.7 1.1 bitcast_dynamic-update-slice_fusion.7
  2.8 1.1 bitcast_dynamic-update-slice_fusion.6
  3.9 1.1 bitcast_dynamic-update-slice_fusion.5
  5.0 1.1 bitcast_dynamic-update-slice_fusion.4
  6.1 1.1 bitcast_dynamic-update-slice_fusion.3
  7.1 1.1 bitcast_dynamic-update-slice_fusion.2
  8.2 1.1 bitcast_dynamic-update-slice_fusion.1
  9.3 54.0 %all_to_all.5 = f32[8,32,4096]{2,1,0:T(8,128)S(1)} all-to-all(f32[8,32,4096]{2,1,0:T(8,128)S(1)} %bitcast_dynamic-update-slice_fusion.1), channel_id=1, replica_groups=mesh['grp'=4,'wr'=8] {'wr'}, dimensions={0} | all-to-all | bytes 8388608 | tf_op jit(solution)/shard_map/all_to_all | solution.py:11
  63.3 0.0 copy-start
  63.3 3.5 %fusion.10 = f32[256,256]{0,1:T(8,128)S(1)} fusion(f32[256,4096]{1,0:T(8,128)S(1)} %bitcast.55), kind=kOutput, calls=%fused_computation.39 | convolution fusion | flops 3221225472 | bytes 4456448 | tf_op jit(solution)/shard_map/dot_general | solution.py:24
  66.9 0.0 copy-done
  66.9 1.6 collective-permute-start
  68.5 5.9 %collective-permute-done = f32[256,256]{0,1:T(8,128)S(1)} collective-permute-done((f32[256,256]{0,1:T(8,128)S(1)}, f32[256,256]{0,1:T(8,128)S(1)}, u32[]{:S(2)}, u32[]{:S(2)}) %collective-permute-start) | collective-permute-done | bytes 262176 | tf_op jit(solution)/shard_map/ppermute | solution.py:20
  74.5 2.7 %collective-permute-start.1 = (f32[256,256]{0,1:T(8,128)S(1)}, f32[256,256]{0,1:T(8,128)S(1)}, u32[]{:S(2)}, u32[]{:S(2)}) collective-permute-start(f32[256,256]{0,1:T(8,128)S(1)} %add.40), channel_id=1, source_target_pairs={{0,16},{8,24},{16,0},{24,8},{1,17},{9,25},{17,1},{25,9},{2,18},{10... | collective-permute-start | bytes 786440 | tf_op jit(solution)/shard_map/ppermute | solution.py:20
  77.1 10.6 %collective-permute-done.1 = f32[256,256]{0,1:T(8,128)S(1)} collective-permute-done((f32[256,256]{0,1:T(8,128)S(1)}, f32[256,256]{0,1:T(8,128)S(1)}, u32[]{:S(2)}, u32[]{:S(2)}) %collective-permute-start.1) | collective-permute-done | bytes 262176 | tf_op jit(solution)/shard_map/ppermute | solution.py:20
  87.7 0.1 collective-permute-start.2
  87.8 1.5 collective-permute-done.2
  89.4 1.8 %collective-permute-start.3 = (f32[256,256]{0,1:T(8,128)S(1)}, f32[256,256]{0,1:T(8,128)S(1)}, u32[]{:S(2)}, u32[]{:S(2)}) collective-permute-start(f32[256,256]{0,1:T(8,128)S(1)} %add.42), channel_id=1, source_target_pairs={{0,2},{1,3},{2,0},{3,1},{4,6},{5,7},{6,4},{7,5},{8,10},{9,11},{10,... | collective-permute-start | bytes 786440 | tf_op jit(solution)/shard_map/ppermute | solution.py:20
  91.2 6.6 %collective-permute-done.3 = f32[256,256]{0,1:T(8,128)S(1)} collective-permute-done((f32[256,256]{0,1:T(8,128)S(1)}, f32[256,256]{0,1:T(8,128)S(1)}, u32[]{:S(2)}, u32[]{:S(2)}) %collective-permute-start.3) | collective-permute-done | bytes 262176 | tf_op jit(solution)/shard_map/ppermute | solution.py:20
  97.9 0.6 collective-permute-start.4
  98.4 4.0 %fusion.9 = (f32[4,32,4096]{2,1,0:T(8,128)}, f32[4,32,4096]{2,1,0:T(8,128)S(1)}) fusion(f32[8,32,4096]{2,1,0:T(8,128)} %copy-done), kind=kLoop, calls=%fused_computation.38 | loop fusion | bytes 8388608 | tf_op jit(solution)/shard_map/triangular_solve | solution.py:52
  102.5 3.0 %collective-permute-done.4 = f32[256,256]{0,1:T(8,128)S(1)} collective-permute-done((f32[256,256]{0,1:T(8,128)S(1)}, f32[256,256]{0,1:T(8,128)S(1)}, u32[]{:S(2)}, u32[]{:S(2)}) %collective-permute-start.4) | collective-permute-done | bytes 262176 | tf_op jit(solution)/shard_map/ppermute | solution.py:20
  105.5 0.1 copy.5
  105.7 11.7 %cholesky.50 = f32[128,128]{1,0:T(8,128)S(1)} custom-call(f32[128,128]{1,0:T(8,128)S(1)} %cholesky.118), custom_call_target="Cholesky" | custom-call | tf_op jit(solution)/shard_map/jit(cholesky)/cholesky | solution.py:49
  117.5 9.8 %custom-call.14 = f32[1,128,128]{1,2,0:T(8,128)S(1)} custom-call(f32[1,128,128]{2,1,0:T(8,128)S(1)} %get-tuple-element.27), custom_call_target="InvertDiagBlocksLowerTriangular" | custom-call | tf_op jit(solution)/shard_map/jit(cholesky)/cholesky | solution.py:49
  127.3 0.2 constant_dynamic-update-slice_fusion
  127.5 0.3 slice_subtract_fusion
  127.8 11.9 %cholesky.105 = f32[128,128]{1,0:T(8,128)S(1)} custom-call(f32[128,128]{1,0:T(8,128)S(1)} %slice_subtract_fusion), custom_call_target="Cholesky" | custom-call | tf_op jit(solution)/shard_map/jit(cholesky)/cholesky | solution.py:49
  139.7 0.6 compare_reduce_fusion
  141.6 0.1 triangular_solve.61
  141.6 3.8 %while.1 = (s32[]{:T(128)}, f32[256,256]{1,0:T(8,128)S(1)}, s32[2,2]{1,0:T(2,128)S(1)}, f32[2,128,128]{2,1,0:T(8,128)S(1)}, s32[]{:T(128)}) while((s32[]{:T(128)}, f32[256,256]{1,0:T(8,128)S(1)}, s32[2,2]{1,0:T(2,128)S(1)}, f32[2,128,128]{2,1,0:T(8,128)S(1)}, s32[]{:T(128)}) %tuple.29), condition=%wide.while_cond, body=%wide.while_body.sunk | while | flops 2 | bytes 131189 | solution.py:52
  141.6 0.6 fusion.19
  142.2 1.3 bitcast_dynamic-update-slice_fusion.10
  143.5 0.6 fusion.19
  144.1 1.3 bitcast_dynamic-update-slice_fusion.10
  145.4 19.7 %custom-call.15 = f32[2,128,128]{1,2,0:T(8,128)S(1)} custom-call(f32[2,128,128]{2,1,0:T(8,128)S(1)} %get-tuple-element.9), custom_call_target="InvertDiagBlocksLowerTriangular" | custom-call | tf_op jit(solution)/shard_map/triangular_solve | solution.py:52
  165.1 3.5 %fusion.4 = f32[128,4096]{1,0:T(8,128)S(1)} fusion(f32[128,4096]{1,0:T(8,128)} %bitcast.57, f32[2,128,128]{1,2,0:T(8,128)S(1)} %custom-call.15), kind=kOutput, calls=%fused_computation.21 | convolution fusion | flops 805306368 | bytes 4259840 | tf_op jit(solution)/shard_map/triangular_solve | solution.py:52
  168.6 2.0 %convolution_subtract_fusion = f32[128,4096]{1,0:T(8,128)S(1)} fusion(f32[128,4096]{1,0:T(8,128)S(1)} %bitcast.56, f32[128,4096]{1,0:T(8,128)S(1)} %fusion.4, f32[256,256]{1,0:T(8,128)S(1)} %get-tuple-element.76), kind=kOutput, calls=%fused_computation.2 | convolution fusion | flops 805830656 | bytes 6356992 | tf_op jit(solution)/shard_map/triangular_solve | solution.py:52
  170.6 1.9 %fusion.3 = f32[128,4096]{1,0:T(8,128)S(1)} fusion(f32[128,4096]{1,0:T(8,128)S(1)} %convolution_subtract_fusion, f32[2,128,128]{1,2,0:T(8,128)S(1)} %custom-call.15), kind=kOutput, calls=%fused_computation.19 | convolution fusion | flops 805306368 | bytes 4259840 | tf_op jit(solution)/shard_map/triangular_solve | solution.py:52
  172.5 2.7 %maximum_multiply_fusion = f32[256,4096]{1,0:T(8,128)} fusion(f32[128,4096]{1,0:T(8,128)S(1)} %fusion.3, f32[128,4096]{1,0:T(8,128)S(1)} %fusion.4), kind=kLoop, calls=%fused_computation.3 | loop fusion | flops 2097152 | bytes 8388608 | tf_op jit(solution)/shard_map/mul | solution.py:56
  175.3 0.6 multiply_bitcast_fusion
  (15 shorter events, 0.4 us)
Async XLA Ops:
  63.3 3.5 %copy-start = (f32[8,32,4096]{2,1,0:T(8,128)}, f32[8,32,4096]{2,1,0:T(8,128)S(1)}, u32[]{:S(2)}) copy-start(f32[8,32,4096]{2,1,0:T(8,128)S(1)} %all_to_all.5) | copy-start | bytes 12582916
  66.9 7.6 %collective-permute-start = (f32[256,256]{0,1:T(8,128)S(1)}, f32[256,256]{0,1:T(8,128)S(1)}, u32[]{:S(2)}, u32[]{:S(2)}) collective-permute-start(f32[256,256]{0,1:T(8,128)S(1)} %fusion.10), channel_id=1, source_target_pairs={{0,8},{8,0},{16,24},{24,16},{1,9},{9,1},{17,25},{25,17},{2,10},{10... | collective-permute-start | bytes 786440 | tf_op jit(solution)/shard_map/ppermute | solution.py:20
  74.5 13.2 %collective-permute-start.1 = (f32[256,256]{0,1:T(8,128)S(1)}, f32[256,256]{0,1:T(8,128)S(1)}, u32[]{:S(2)}, u32[]{:S(2)}) collective-permute-start(f32[256,256]{0,1:T(8,128)S(1)} %add.40), channel_id=1, source_target_pairs={{0,16},{8,24},{16,0},{24,8},{1,17},{9,25},{17,1},{25,9},{2,18},{10... | collective-permute-start | bytes 786440 | tf_op jit(solution)/shard_map/ppermute | solution.py:20
  87.7 1.6 collective-permute-start.2
  89.4 8.5 %collective-permute-start.3 = (f32[256,256]{0,1:T(8,128)S(1)}, f32[256,256]{0,1:T(8,128)S(1)}, u32[]{:S(2)}, u32[]{:S(2)}) collective-permute-start(f32[256,256]{0,1:T(8,128)S(1)} %add.42), channel_id=1, source_target_pairs={{0,2},{1,3},{2,0},{3,1},{4,6},{5,7},{6,4},{7,5},{8,10},{9,11},{10,... | collective-permute-start | bytes 786440 | tf_op jit(solution)/shard_map/ppermute | solution.py:20
  97.9 7.6 %collective-permute-start.4 = (f32[256,256]{0,1:T(8,128)S(1)}, f32[256,256]{0,1:T(8,128)S(1)}, u32[]{:S(2)}, u32[]{:S(2)}) collective-permute-start(f32[256,256]{0,1:T(8,128)S(1)} %add.43), channel_id=1, source_target_pairs={{0,4},{1,5},{2,6},{3,7},{4,0},{5,1},{6,2},{7,3},{8,12},{9,13},{10,... | collective-permute-start | bytes 786440 | tf_op jit(solution)/shard_map/ppermute | solution.py:20
